TPU v7x, 32 devices: a whole 2x2x4 slice. The times are simulated.
32 devices in a mesh: strip: 8 (over z, x), seq: 4 (over y, core).
Axes of the slice: x: 2, y: 2, z: 4, core: 2. Of those that a mesh axis runs over, the one named last changes fastest.
Arguments:
- slide_image: bfloat16 [3, 256, 4096], P(None, 'strip', 'seq'), may hold values from -6 to 6
- keep_flags: int32 [16, 256], P('strip', 'seq'), may hold values from 0 to 1, as said below
- owner_shift: int32 [4], P('seq'), may hold values from 0 to 7
- weight_one: bfloat16 [9, 64, 3], replicated, may hold values from -1.25 to 1.25
- offset_one: float32 [64], replicated, may hold values from -3 to 3
- weight_two: bfloat16 [9, 128, 64], replicated, may hold values from -0.25 to 0.25
- offset_two: float32 [128], replicated, may hold values from -3 to 3
- weight_three: bfloat16 [9, 256, 128], replicated, may hold values from -0.1875 to 0.1875
- offset_three: float32 [256], replicated, may hold values from -3 to 3
- patch_weight: bfloat16 [4, 256, 1536], replicated, may hold values from -0.1875 to 0.1875
- patch_offset: float32 [1536], replicated, may hold values from -3 to 3
Outputs:
- sequences: bfloat16 [4, 512, 1536], P('seq', 'strip')
Inputs may be any that keep to these rules, and one draw needn't show every extreme that they name: `keep_flags`: exactly half of the patches of each band are kept; some device of each band keeps all 128 of its patches and another keeps none.
All inputs are finite; a program needn't handle non-finite values.
Results may differ from a plain program's by a relative error of at most 0.0049.
Values may be sent and summed in bfloat16 or wider, within the bound.
A program may use at most 128 MiB of HBM per device.

v0:
```python
import functools

import jax
import jax.numpy as jnp
from jax import lax
from jax.experimental import pallas as pl
from jax.experimental.pallas import tpu as pltpu
from jax.sharding import PartitionSpec as P

MESH = pl.DeviceIdType.MESH
F32 = jnp.float32
BF16 = jnp.bfloat16

M1 = 560
M2 = 272
M3 = 128


def gelu(x):
    return 0.5 * x * (1.0 + lax.erf(x * 0.7071067811865476))


def rounded(x):
    return x.astype(BF16).astype(F32)


def dot(a, b):
    return jnp.dot(a, b, preferred_element_type=F32)


def dot_nt(a, b):
    return lax.dot_general(a, b, (((1,), (1,)), ((), ())), preferred_element_type=F32)


def kernel(
    n, n_seq, cap,
    shift_ref, img_hbm, flag_hbm, w1_hbm, b1_hbm, w2_hbm, b2_hbm, w3_hbm, b3_hbm, pw_hbm, pb_hbm,
    out_ref,
    img_ref, flag_ref, w1_ref, b1_ref, w2_ref, b2_ref, w3_ref, b3_ref, pw, pb_ref, top, left, corner, flags, slab, slab_t, a1, k1, s1, s2, s3, sendbuf, got,
    halo_send, halo_recv, flag_send, flag_recv, row_send, row_recv, load_sem,
):
    me = lax.axis_index("strip")
    mq = lax.axis_index("seq")
    down, up = lax.rem(me + 1, n), lax.rem(me + n - 1, n)
    right, leftward = lax.rem(mq + 1, n_seq), lax.rem(mq + n_seq - 1, n_seq)

    loads = [
        pltpu.make_async_copy(src, dst, load_sem.at[k])
        for k, (src, dst) in enumerate(
            (
                (flag_hbm, flag_ref), (img_hbm, img_ref), (w1_hbm, w1_ref), (b1_hbm, b1_ref),
                (w2_hbm, w2_ref), (b2_hbm, b2_ref), (w3_hbm, w3_ref), (b3_hbm, b3_ref),
                (pb_hbm, pb_ref), (pw_hbm, pw),
            )
        )
    ]
    w3_copy, pw_copy = loads[6], loads[9]
    barrier = pltpu.get_barrier_semaphore()

    def greet(i, c):
        pl.semaphore_signal(barrier, inc=1, device_id=(lax.rem(me + i, n), mq), device_id_type=MESH)
        return c

    lax.fori_loop(1, n, greet, 0)
    for where in ((me, right), (me, leftward), (down, right), (up, leftward)):
        pl.semaphore_signal(barrier, inc=1, device_id=where, device_id_type=MESH)

    for load in loads[:9]:
        load.start()
    pl.semaphore_wait(barrier, n - 1 + 4)

    def flag_copy(i, source):
        return pltpu.make_async_remote_copy(
            src_ref=flag_hbm, dst_ref=flags.at[source],
            send_sem=flag_send.at[i], recv_sem=flag_recv.at[i],
            device_id=(lax.rem(me + i, n), mq), device_id_type=MESH,
        )

    halos = [
        pltpu.make_async_remote_copy(
            src_ref=src, dst_ref=dst, send_sem=halo_send.at[k], recv_sem=halo_recv.at[k],
            device_id=where, device_id_type=MESH,
        )
        for k, (src, dst, where) in enumerate(
            (
                (img_hbm.at[:, 24:32, :], top, (down, mq)),
                (img_hbm.at[:, :, 896:1024], left, (me, right)),
                (img_hbm.at[:, 24:32, 896:1024], corner, (down, right)),
            )
        )
    ]
    inner_row = me > 0
    inner_col = mq > 0
    to_down, to_right = me < n - 1, mq < n_seq - 1
    sends = (to_down, to_right, jnp.logical_and(to_down, to_right))
    receives = (inner_row, inner_col, jnp.logical_and(inner_row, inner_col))
    for halo, sent in zip(halos, sends):
        pl.when(sent)(halo.start)

    def send_flags(i, c):
        flag_copy(i, me).start()
        return c

    lax.fori_loop(1, n, send_flags, 0)
    pw_copy.start()
    for load in loads[:6] + loads[7:9]:
        load.wait()
    flags[me] = flag_ref[...]
    sub = lax.broadcasted_iota(jnp.int32, (128, 128), 0)
    lane = lax.broadcasted_iota(jnp.int32, (128, 128), 1)
    row_in = sub - jnp.where(sub >= 80, 80, jnp.where(sub >= 40, 40, 0))
    tap0 = jnp.where(sub < 120, row_in - 1 - 2 * jnp.where(lane >= 64, 1, 0), -1000)
    for dx in range(3):
        spread = []
        for dy in range(3):
            tap_w = w1_ref[3 * dy + dx].astype(F32)
            tap_w = jnp.concatenate([tap_w, tap_w], axis=1)
            parts = [jnp.broadcast_to(tap_w[c : c + 1], (40, 128)) for c in range(3)]
            spread.append(jnp.concatenate(parts + [jnp.zeros((8, 128), F32)], axis=0))
        for q in range(10):
            tap = tap0 - 4 * q
            band = jnp.where(
                tap == 0,
                spread[0],
                jnp.where(tap == 1, spread[1], jnp.where(tap == 2, spread[2], 0.0)),
            )
            k1[128 * dx : 128 * dx + 128, 128 * q : 128 * q + 128] = band.astype(BF16)


    slab[120:128, :] = jnp.zeros((8, 1152), F32)
    for c in range(3):
        slab[40 * c + 8 : 40 * c + 40, 128:1152] = img_ref[c].astype(F32)
    for buf, sent, received, halo in zip((top, left, corner), sends, receives, halos):
        pl.when(received)(halo.wait_recv)

        @pl.when(jnp.logical_not(received))
        def _(buf=buf):
            buf[...] = jnp.zeros_like(buf)

    for c in range(3):
        slab[40 * c : 40 * c + 8, 128:1152] = top[c].astype(F32)
        slab[40 * c + 8 : 40 * c + 40, 0:128] = left[c].astype(F32)
        slab[40 * c : 40 * c + 8, 0:128] = corner[c].astype(F32)
    for t in range(9):
        slab_t[128 * t : 128 * t + 128, :] = slab[:, 128 * t : 128 * t + 128].T
    slab_t[1152:1280, :] = jnp.zeros((128, 128), F32)
    for dx in range(3):
        a1[:, 128 * dx : 128 * dx + 128] = slab_t[pl.ds(119 + dx, M1, stride=2), :].astype(BF16)

    sub1 = lax.broadcasted_iota(jnp.int32, (M1, 256), 0)
    lane1 = lax.broadcasted_iota(jnp.int32, (M1, 256), 1)
    col_ok1 = jnp.logical_or(inner_col, sub1 >= 4)
    b1 = jnp.concatenate([b1_ref[...]] * 4, axis=1)

    def layer_one(t):
        summed = dot(a1[...], k1[:, 256 * t : 256 * t + 256])
        act = gelu(summed + b1)
        ok = col_ok1
        if t == 0:
            ok = jnp.logical_and(ok, jnp.logical_or(inner_row, lane1 >= 192))
        act = rounded(jnp.where(ok, act, 0.0))
        s1[2 * t] = act[:, :128]
        s1[2 * t + 1] = act[:, 128:]

    sub2 = lax.broadcasted_iota(jnp.int32, (M2, 128), 0)
    col_ok2 = jnp.logical_or(inner_col, sub2 >= 1)
    w2 = [
        jnp.concatenate(
            [w2_ref[dx], w2_ref[3 + dx], w2_ref[6 + dx], jnp.zeros((64, 128), BF16)], axis=0
        )
        for dx in range(3)
    ]

    def layer_two(r, c):
        summed = None
        for dx in range(3):
            a = jnp.concatenate(
                [s1[r + h, pl.ds(1 + dx, M2, stride=2), :].astype(BF16) for h in range(2)], axis=1
            )
            part = dot(a, w2[dx])
            summed = part if summed is None else summed + part
        act = gelu(summed + b2_ref[...])
        ok = jnp.logical_and(col_ok2, jnp.logical_or(inner_row, r > 0))
        s2[r] = rounded(jnp.where(ok, act, 0.0))
        return c

    def layer_three(r, c):
        summed = None
        for dy in range(3):
            for dx in range(3):
                a = s2[2 * r + dy, pl.ds(dx, M3, stride=2), :].astype(BF16)
                part = dot_nt(a, w3_ref[3 * dy + dx])
                summed = part if summed is None else summed + part
        act = rounded(gelu(summed + b3_ref[...]))
        s3[0, r] = act[:, :128]
        s3[1, r] = act[:, 128:]
        return c

    def wait_flags(i, c):
        flag_copy(i, lax.rem(me + n - i, n)).wait()
        return c

    lax.fori_loop(1, n, wait_flags, 0)
    bits = n.bit_length() - 1
    cap_bits = cap.bit_length() - 1
    places = n * cap
    own = out_ref.shape[0]
    shift = shift_ref[0]
    src_of = lax.broadcasted_iota(jnp.int32, (n, places), 1) >> cap_bits
    src_at = lax.broadcasted_iota(jnp.int32, (n, places), 0)
    same = jnp.where(src_at == src_of, 1.0, 0.0).astype(BF16)
    earlier = jnp.where(src_at < src_of, 1.0, 0.0).astype(BF16)
    n_lane = lax.broadcasted_iota(jnp.int32, (8, n), 1)
    turn = lax.broadcasted_iota(jnp.int32, (1, places), 1) & (cap - 1)
    slots = lax.broadcasted_iota(jnp.int32, (own, places), 0)
    spot = lax.broadcasted_iota(jnp.int32, (places, 1), 0)
    upper = jnp.where(
        lax.broadcasted_iota(jnp.int32, (64, 64), 0) < lax.broadcasted_iota(jnp.int32, (64, 64), 1),
        1.0, 0.0,
    ).astype(BF16)
    counts = [
        dot_nt(jnp.ones((8, 64), BF16), flags[:, pr, :].astype(F32).astype(BF16)).astype(BF16)
        for pr in range(2)
    ]
    count_l = [dot(part, same)[0:1].astype(jnp.int32) for part in counts]
    start_l = dot(counts[0], earlier)[0:1] + dot(counts[1], earlier)[0:1]
    start_l = start_l.astype(jnp.int32)
    total = counts[0].astype(F32) + counts[1].astype(F32)
    my_start = jnp.sum(jnp.where(n_lane < me, total, 0.0), axis=1, keepdims=True)[0:1]
    place, pick = [], []
    for pr in range(2):
        rank_l = ((me - shift - start_l) & (n - 1)) + n * turn
        slot_l = jnp.where(rank_l < count_l[pr], (start_l + rank_l) >> bits, -1)
        place.append(jnp.where(slots == slot_l, 1.0, 0.0).astype(BF16))
        row = flag_ref[pr : pr + 1].astype(F32)
        within = dot(jnp.broadcast_to(row, (16, 64)).astype(BF16), upper)[0:1]
        rank = jnp.where(row > 0.5, within, -1.0).astype(jnp.int32)
        first = my_start.astype(jnp.int32)
        wanted = (((spot >> cap_bits) - shift - first) & (n - 1)) + n * (spot & (cap - 1))
        pick.append(jnp.where(rank == wanted, 1.0, 0.0).astype(BF16))
        start_l = start_l + count_l[pr]
        my_start = my_start + jnp.sum(row, axis=1, keepdims=True)

    def row_copy(pr, i, source):
        return pltpu.make_async_remote_copy(
            src_ref=sendbuf.at[pr, lax.rem(me + i, n)], dst_ref=got.at[pr, source],
            send_sem=row_send.at[pr, i], recv_sem=row_recv.at[pr, i],
            device_id=(lax.rem(me + i, n), mq), device_id_type=MESH,
        )

    for pr in range(2):
        for t in range(3 * pr, 3 + 2 * pr):
            layer_one(t)
        lax.fori_loop(5 * pr, 5 + 4 * pr, layer_two, 0)
        if pr == 0:
            w3_copy.wait()
        lax.fori_loop(2 * pr, 2 * pr + 2, layer_three, 0)
        features = jnp.concatenate(
            [
                s3[h, 2 * pr + a, pl.ds(b, 64, stride=2), :].astype(BF16)
                for a in range(2) for b in range(2) for h in range(2)
            ],
            axis=1,
        )
        rows = dot(pick[pr], features)
        sendbuf[pr] = rows.reshape(n, cap, rows.shape[1]).astype(BF16)

        def send_rows(i, c, pr=pr):
            row_copy(pr, i, me).start()
            return c

        lax.fori_loop(1, n, send_rows, 0)
        got[pr, me] = sendbuf[pr, me]

    pw_copy.wait()
    placed = None
    for pr in range(2):

        def wait_rows(i, c, pr=pr):
            row_copy(pr, i, lax.rem(me + n - i, n)).wait()
            return c

        lax.fori_loop(1, n, wait_rows, 0)
        rows = got[pr].astype(F32).reshape(places, 1024).astype(BF16)
        part = dot(place[pr], rows)
        placed = part if placed is None else placed + part
    placed = placed.astype(BF16)
    filled = jnp.sum(place[0].astype(F32), axis=1, keepdims=True)
    filled = filled + jnp.sum(place[1].astype(F32), axis=1, keepdims=True)
    for t in range(6):
        cut = slice(256 * t, 256 * t + 256)
        summed = None
        for k in range(4):
            part = dot(placed[:, 256 * k : 256 * k + 256], pw[k, :, cut])
            summed = part if summed is None else summed + part
        bias = jnp.concatenate([pb_ref[2 * t : 2 * t + 1], pb_ref[2 * t + 1 : 2 * t + 2]], axis=1)
        out_ref[:, cut] = jnp.where(filled > 0.5, summed + bias, 0.0).astype(BF16)
    for halo, sent in zip(halos, sends):
        pl.when(sent)(halo.wait_send)


def local(n, n_seq, slide_image, keep_flags, owner_shift, weight_one, offset_one, weight_two,
          offset_two, weight_three, offset_three, patch_weight, patch_offset):
    patches = keep_flags.size
    embed = patch_weight.shape[2]
    cap = 8 * -(-(-(-keep_flags.shape[1] // n)) // 8)
    width = patch_weight.shape[0] * patch_weight.shape[1]
    arrays = (
        slide_image, keep_flags, weight_one.transpose(0, 2, 1), offset_one[None],
        weight_two.transpose(0, 2, 1), offset_two[None], weight_three, offset_three[None],
        patch_weight, patch_offset.reshape(-1, 128),
    )
    vmem = pl.BlockSpec(memory_space=pltpu.VMEM)
    anywhere = pl.BlockSpec(memory_space=pl.ANY)
    dma = pltpu.SemaphoreType.DMA
    placed = pl.pallas_call(
        functools.partial(kernel, n, n_seq, cap),
        name="stem_and_deal",
        out_shape=jax.ShapeDtypeStruct((patches // 2, embed), BF16),
        in_specs=[pl.BlockSpec(memory_space=pltpu.SMEM)] + [anywhere] * 10,
        out_specs=vmem,
        scratch_shapes=[
            *(pltpu.VMEM(x.shape, x.dtype) for x in arrays),
            pltpu.VMEM((3, 8, 1024), BF16),
            pltpu.VMEM((3, 32, 128), BF16),
            pltpu.VMEM((3, 8, 128), BF16),
            pltpu.VMEM((n,) + keep_flags.shape, jnp.int32),
            pltpu.VMEM((128, 1152), F32),
            pltpu.VMEM((1280, 128), F32),
            pltpu.VMEM((M1, 384), BF16),
            pltpu.VMEM((384, 1280), BF16),
            pltpu.VMEM((10, M1, 128), F32),
            pltpu.VMEM((9, M2, 128), F32),
            pltpu.VMEM((2, 4, M3, 128), F32),
            pltpu.VMEM((2, n, cap, width), BF16),
            pltpu.VMEM((2, n, cap, width), BF16),
            dma((3,)), dma((3,)), dma((n,)), dma((n,)), dma((2, n)), dma((2, n)), dma((10,)),
        ],
        compiler_params=pltpu.CompilerParams(
            collective_id=0, has_side_effects=True, vmem_limit_bytes=60000000
        ),
    )(
        owner_shift, *arrays,
    )
    return placed[None]


def solution(mesh):
    args = (P(None, "strip", "seq"), P("strip", "seq"), P("seq")) + (P(),) * 8
    return jax.shard_map(
        functools.partial(local, mesh.shape["strip"], mesh.shape["seq"]),
        mesh=mesh, in_specs=args, out_specs=P("seq", "strip", None), check_vma=False,
    )
```

profile of v0, /device:TPU:0, one launch (start us, length us, event | category | flops | bytes accessed | tf_op | source)
XLA Modules:
  0.0 25.2 jit_solution(11735862873916201867)
XLA Ops:
  0.7 22.9 %stem_and_deal.1 = bf16[64,1536]{1,0:T(8,128)(2,1)} custom-call(s32[1]{0:T(128)S(6)} %copy.13.shift_ref, bf16[3,32,1024]{2,1,0:T(8,128)(2,1)} %img_hbm.1, s32[2,64]{1,0:T(2,128)} %flag_hbm.1, bf16[9,3,64]{2,1,0:T(4,128)(2,1)} %bitcast.9, f32[1,64]{1,0:T(1,128)} %bitcast.12, bf16[9,64,128]{2,1,0:T(8,128)(2,1)} %bitcast.8, f32[1,128]{1,0:T(1,128)} %bitcast.13, ...), custom_call_target="tpu_custom_call" | custom-call | tf_op jit(solution)/shard_map/stem_and_deal/pallas_call | solution.py:316
  23.6 1.6 %copy.14 = bf16[1,64,1536]{2,1,0:T(8,128)(2,1)} copy(bf16[1,64,1536]{2,1,0:T(8,128)(2,1)} %bitcast.7) | data formatting | bytes 393216
where the time goes:
time: 25.3 us; the launch traced here: 25.2 us
  Pallas kernels  22.9 us (91%)
  local copies, waits for them, and re-layouts  1.62 us (6%)
  between operations  0.66 us (3%)
    pallas_call x1, Pallas kernels, local(): pl.pallas_call(functools.partial(kernel, n, n_seq, cap), name='stem_and_d...  22.9 us
    unnamed x1, local copies, waits for them, and re-layouts  1.62 us

commit v1 on v0

v1 whole, which is shorter than its diff:
```python
import functools

import jax
import jax.numpy as jnp
from jax import lax
from jax.experimental import pallas as pl
from jax.experimental.pallas import tpu as pltpu
from jax.sharding import PartitionSpec as P

MESH = pl.DeviceIdType.MESH
F32 = jnp.float32
BF16 = jnp.bfloat16

M1 = 560
M2 = 272
M3 = 128
VMEM1 = 60000000


def gelu(x):
    return 0.5 * x * (1.0 + lax.erf(x * 0.7071067811865476))


def dot(a, b):
    return jnp.dot(a, b, preferred_element_type=F32)


def dot_nt(a, b):
    return lax.dot_general(a, b, (((1,), (1,)), ((), ())), preferred_element_type=F32)


def kernel(
    n, n_seq, cap,
    shift_ref, img_hbm, flag_hbm, w1_hbm, b1_hbm, w2_hbm, b2_hbm, w3_hbm, b3_hbm, pw_hbm,
    out_ref, pw_out,
    img_ref, flag_ref, w1_ref, b1_ref, w2_ref, b2_ref, w3_ref, b3_ref, top, left, corner, flags, band, slab, slab_t, a1, k1, s1, s2, s3, sendbuf, got,
    halo_send, halo_recv, flag_send, flag_recv, row_send, row_recv, load_sem, pw_sem,
):
    me = lax.axis_index("strip")
    mq = lax.axis_index("seq")
    half = n // 2
    late = me // half
    down, up = lax.rem(me + 1, n), lax.rem(me + n - 1, n)
    right, leftward = lax.rem(mq + 1, n_seq), lax.rem(mq + n_seq - 1, n_seq)

    loads = [
        pltpu.make_async_copy(src, dst, load_sem.at[k])
        for k, (src, dst) in enumerate(
            (
                (w1_hbm, w1_ref), (img_hbm, img_ref), (b1_hbm, b1_ref), (w2_hbm, w2_ref),
                (b2_hbm, b2_ref), (w3_hbm, w3_ref), (b3_hbm, b3_ref), (flag_hbm, flag_ref),
            )
        )
    ]
    barrier = pltpu.get_barrier_semaphore()

    def greet(i, c):
        pl.semaphore_signal(barrier, inc=1, device_id=(lax.rem(me + i, n), mq), device_id_type=MESH)
        return c

    for load in loads[:2]:
        load.start()
    for where in ((me, right), (me, leftward), (down, right), (up, leftward)):
        pl.semaphore_signal(barrier, inc=1, device_id=where, device_id_type=MESH)
    lax.fori_loop(1, n, greet, 0)
    for load in loads[2:]:
        load.start()

    pw_copy = pltpu.make_async_copy(pw_hbm, pw_out, pw_sem)

    def flag_copy(i, source):
        return pltpu.make_async_remote_copy(
            src_ref=flag_hbm, dst_ref=flags.at[source],
            send_sem=flag_send.at[i], recv_sem=flag_recv.at[i],
            device_id=(lax.rem(me + i, n), mq), device_id_type=MESH,
        )

    halos = [
        pltpu.make_async_remote_copy(
            src_ref=src, dst_ref=dst, send_sem=halo_send.at[k], recv_sem=halo_recv.at[k],
            device_id=where, device_id_type=MESH,
        )
        for k, (src, dst, where) in enumerate(
            (
                (img_ref.at[:, 24:32, :], top, (down, mq)),
                (img_ref.at[:, :, 896:1024], left, (me, right)),
                (img_ref.at[:, 24:32, 896:1024], corner, (down, right)),
            )
        )
    ]
    inner_row = me > 0
    inner_col = mq > 0
    to_down, to_right = me < n - 1, mq < n_seq - 1
    sends = (to_down, to_right, jnp.logical_and(to_down, to_right))
    receives = (inner_row, inner_col, jnp.logical_and(inner_row, inner_col))

    def send_flags(i, c):
        flag_copy(i, me).start()
        return c

    def enter():
        pl.semaphore_wait(barrier, n - 1 + 4)
        for halo, sent in zip(halos, sends):
            pl.when(sent)(halo.start)
        lax.fori_loop(1, n, send_flags, 0)

    loads[0].wait()
    low = lax.broadcasted_iota(jnp.int32, (8, 128), 0)
    low_lane = lax.broadcasted_iota(jnp.int32, (8, 128), 1)
    tap = low - 1 - 2 * jnp.where(low_lane >= 64, 1, 0)
    band[...] = jnp.zeros_like(band)
    for dx in range(3):
        tap_w = [w1_ref[3 * dy + dx].astype(F32) for dy in range(3)]
        tap_w = [jnp.concatenate([w, w], axis=1) for w in tap_w]
        for c in range(3):
            block = jnp.zeros((8, 128), F32)
            for dy in range(3):
                block = jnp.where(tap == dy, jnp.broadcast_to(tap_w[dy][c : c + 1], (8, 128)), block)
            band[dx, c, 40:48, :] = block
        for q in range(10):
            parts = [band[dx, c, 40 - 4 * q : 80 - 4 * q, :] for c in range(3)]
            parts = jnp.concatenate(parts + [jnp.zeros((8, 128), F32)], axis=0)
            k1[128 * dx : 128 * dx + 128, 128 * q : 128 * q + 128] = parts.astype(BF16)

    slab[120:128, :] = jnp.zeros((8, 1152), F32)
    slab[:120, 0:128] = jnp.zeros((120, 128), F32)
    loads[1].wait()
    for c in range(3):
        slab[40 * c : 40 * c + 8, 128:1152] = jnp.zeros((8, 1024), F32)
        slab[40 * c + 8 : 40 * c + 40, 128:1152] = img_ref[c].astype(F32)
    slab_t[1152:1280, :] = jnp.zeros((128, 128), F32)

    def fill_a1():
        for t in range(9):
            slab_t[128 * t : 128 * t + 128, :] = slab[:, 128 * t : 128 * t + 128].T
        for dx in range(3):
            a1[:, 128 * dx : 128 * dx + 128] = slab_t[pl.ds(119 + dx, M1, stride=2), :].astype(BF16)

    fill_a1()
    loads[2].wait()
    b1 = jnp.concatenate([b1_ref[...]] * 4, axis=1)

    def layer_one(t, rows):
        act = gelu(dot(a1[:rows], k1[:, 256 * t : 256 * t + 256]) + b1)
        if t == 0 or rows < M1:
            sub1 = lax.broadcasted_iota(jnp.int32, (rows, 256), 0)
            ok = jnp.logical_or(inner_col, sub1 >= 4)
            if t == 0:
                lane1 = lax.broadcasted_iota(jnp.int32, (rows, 256), 1)
                ok = jnp.logical_and(ok, jnp.logical_or(inner_row, lane1 >= 192))
            act = jnp.where(ok, act, 0.0)
        s1[2 * t, :rows] = act[:, :128]
        s1[2 * t + 1, :rows] = act[:, 128:]

    def layer_two(where, rows):
        summed = None
        for dx in range(3):
            a = jnp.concatenate(
                [
                    jnp.concatenate(
                        [s1[r + h, pl.ds(1 + dx, rows, stride=2), :] for r in where], axis=0
                    ).astype(BF16)
                    for h in range(2)
                ],
                axis=1,
            )
            w2 = jnp.concatenate(
                [w2_ref[dx], w2_ref[3 + dx], w2_ref[6 + dx], jnp.zeros((64, 128), BF16)], axis=0
            )
            part = dot(a, w2)
            summed = part if summed is None else summed + part
        act = gelu(summed + b2_ref[...])
        sub2 = lax.broadcasted_iota(jnp.int32, (rows, 128), 0)
        col_ok2 = jnp.logical_or(inner_col, sub2 >= 1)
        for k, r in enumerate(where):
            one = act[rows * k : rows * k + rows]
            if r < 2 or rows < M2:
                ok = jnp.logical_and(col_ok2, inner_row) if r == 0 else col_ok2
                one = jnp.where(ok, one, 0.0)
            s2[r, :rows] = one

    def layer_three(where, rows):
        summed = None
        for dy in range(3):
            for dx in range(3):
                a = jnp.concatenate(
                    [s2[2 * r + dy, pl.ds(dx, rows, stride=2), :] for r in where], axis=0
                ).astype(BF16)
                part = dot_nt(a, w3_ref[3 * dy + dx])
                summed = part if summed is None else summed + part
        act = gelu(summed + b3_ref[...])
        for k, r in enumerate(where):
            s3[0, r, :rows] = act[rows * k : rows * k + rows, :128]
            s3[1, r, :rows] = act[rows * k : rows * k + rows, 128:]

    for t in range(1, 5):
        layer_one(t, M1)
    pl.when(late == 1)(enter)
    for load in loads[3:]:
        load.wait()
    pw_copy.start()
    for r in range(4, 9):
        layer_two([r], M2)
    for r in (2, 3):
        layer_three([r], M3)
    pl.when(late == 0)(enter)
    for r in (2, 3):
        layer_two([r], M2)
    layer_three([1], M3)

    for buf, received, halo in zip((top, left, corner), receives, halos):
        pl.when(received)(halo.wait_recv)

        @pl.when(jnp.logical_not(received))
        def _(buf=buf):
            buf[...] = jnp.zeros_like(buf)

    for c in range(3):
        slab[40 * c : 40 * c + 8, 128:1152] = top[c].astype(F32)
        slab[40 * c + 8 : 40 * c + 40, 0:128] = left[c].astype(F32)
        slab[40 * c : 40 * c + 8, 0:128] = corner[c].astype(F32)
    fill_a1()

    flags[me] = flag_ref[...]
    own = out_ref.shape[0]
    places = n * cap
    bits = n.bit_length() - 1
    cap_bits = cap.bit_length() - 1
    shift = shift_ref[0]

    def near_flags(i, c):
        source = lax.rem(me + n - i, n)
        flag_copy(i, source).wait()
        return c + flags[source]

    def far_flags(i, c):
        flag_copy(i, lax.rem(me + n - i, n)).wait()
        return c

    def row_copy(pr, i, source):
        return pltpu.make_async_remote_copy(
            src_ref=sendbuf.at[pr, lax.rem(me + i, n)], dst_ref=got.at[pr, source],
            send_sem=row_send.at[pr, i], recv_sem=row_recv.at[pr, i],
            device_id=(lax.rem(me + i, n), mq), device_id_type=MESH,
        )

    def deal(pr, first):
        spot = lax.broadcasted_iota(jnp.int32, (places, 1), 0)
        upper = jnp.where(
            lax.broadcasted_iota(jnp.int32, (64, 64), 0) < lax.broadcasted_iota(jnp.int32, (64, 64), 1),
            1.0, 0.0,
        ).astype(BF16)
        row = flag_ref[pr : pr + 1].astype(F32)
        within = dot(jnp.broadcast_to(row, (16, 64)).astype(BF16), upper)[0:1]
        rank = jnp.where(row > 0.5, within, -1.0).astype(jnp.int32)
        wanted = (((spot >> cap_bits) - shift - first) & (n - 1)) + n * (spot & (cap - 1))
        pick = jnp.where(rank == wanted, 1.0, 0.0).astype(BF16)
        features = jnp.concatenate(
            [
                s3[h, 2 * pr + a, pl.ds(b, 64, stride=2), :].astype(BF16)
                for a in range(2) for b in range(2) for h in range(2)
            ],
            axis=1,
        )
        rows = dot(pick, features)
        sendbuf[pr] = rows.reshape(n, cap, rows.shape[1]).astype(BF16)

        def send_rows(i, c):
            row_copy(pr, i, me).start()
            return c

        lax.fori_loop(1, n, send_rows, 0)
        got[pr, me] = sendbuf[pr, me]

    for t in range(1, 5):
        layer_one(t, 16)
    layer_two(list(range(4, 9)), 8)
    layer_three([2, 3], 8)
    near = lax.fori_loop(
        1 + late * me, me + 1 + late * (n - me - 1), near_flags, jnp.zeros(flag_ref.shape, jnp.int32)
    )
    near = jnp.sum(near.astype(F32))
    mine = [jnp.sum(flag_ref[pr : pr + 1].astype(F32), axis=1, keepdims=True) for pr in range(2)]
    start = jnp.where(late == 1, n * own - near - mine[0] - mine[1], near + jnp.zeros((1, 1), F32))
    deal(1, (start + mine[0]).astype(jnp.int32))

    layer_one(0, M1)
    layer_two([0], M2)
    layer_two([1], M2)
    layer_two([2, 3], 8)
    layer_three([0], M3)
    layer_three([1], 8)
    deal(0, start.astype(jnp.int32))

    lax.fori_loop(me + 1 - late * me, n - late * (n - me - 1), far_flags, 0)
    src_of = lax.broadcasted_iota(jnp.int32, (n, places), 1) >> cap_bits
    src_at = lax.broadcasted_iota(jnp.int32, (n, places), 0)
    same = jnp.where(src_at == src_of, 1.0, 0.0).astype(BF16)
    earlier = jnp.where(src_at < src_of, 1.0, 0.0).astype(BF16)
    turn = lax.broadcasted_iota(jnp.int32, (1, places), 1) & (cap - 1)
    slots = lax.broadcasted_iota(jnp.int32, (own, places), 0)
    counts = [
        dot_nt(jnp.ones((8, 64), BF16), flags[:, pr, :].astype(F32).astype(BF16)).astype(BF16)
        for pr in range(2)
    ]
    count_l = [dot(part, same)[0:1].astype(jnp.int32) for part in counts]
    start_l = dot(counts[0], earlier)[0:1] + dot(counts[1], earlier)[0:1]
    start_l = start_l.astype(jnp.int32)
    place = []
    for pr in range(2):
        rank_l = ((me - shift - start_l) & (n - 1)) + n * turn
        slot_l = jnp.where(rank_l < count_l[pr], (start_l + rank_l) >> bits, -1)
        place.append(jnp.where(slots == slot_l, 1.0, 0.0).astype(BF16))
        start_l = start_l + count_l[pr]
    filled = jnp.sum(place[0].astype(F32), axis=1, keepdims=True)
    filled = filled + jnp.sum(place[1].astype(F32), axis=1, keepdims=True)
    width = got.shape[3]
    out_ref[:, width:] = jnp.broadcast_to(filled, (own, 128)).astype(BF16)

    placed = None
    for pr in (1, 0):

        def wait_rows(i, c, pr=pr):
            row_copy(pr, i, lax.rem(me + n - i, n)).wait()
            return c

        lax.fori_loop(1, n, wait_rows, 0)
        rows = got[pr].astype(F32).reshape(places, width).astype(BF16)
        part = dot(place[pr], rows)
        placed = part if placed is None else placed + part
    out_ref[:, :width] = placed.astype(BF16)
    for halo, sent in zip(halos, sends):
        pl.when(sent)(halo.wait_send)
    pw_copy.wait()


def project(dealt_ref, pw_ref, pb_ref, out_ref):
    width = pw_ref.shape[0] * pw_ref.shape[1]
    filled = dealt_ref[:, width:].astype(F32)
    filled = jnp.concatenate([filled, filled], axis=1)
    for t in range(6):
        cut = slice(256 * t, 256 * t + 256)
        summed = None
        for k in range(4):
            part = dot(dealt_ref[:, 256 * k : 256 * k + 256], pw_ref[k, :, cut])
            summed = part if summed is None else summed + part
        bias = jnp.concatenate([pb_ref[2 * t : 2 * t + 1], pb_ref[2 * t + 1 : 2 * t + 2]], axis=1)
        out_ref[:, cut] = jnp.where(filled > 0.5, summed + bias, 0.0).astype(BF16)


def local(n, n_seq, slide_image, keep_flags, owner_shift, weight_one, offset_one, weight_two,
          offset_two, weight_three, offset_three, patch_weight, patch_offset):
    patches = keep_flags.size
    embed = patch_weight.shape[2]
    cap = 8 * -(-(-(-keep_flags.shape[1] // n)) // 8)
    width = patch_weight.shape[0] * patch_weight.shape[1]
    arrays = (
        slide_image, keep_flags, weight_one.transpose(0, 2, 1), offset_one[None],
        weight_two.transpose(0, 2, 1), offset_two[None], weight_three, offset_three[None],
    )
    own = patches // 2
    vmem = pl.BlockSpec(memory_space=pltpu.VMEM)
    anywhere = pl.BlockSpec(memory_space=pltpu.HBM)
    dma = pltpu.SemaphoreType.DMA
    dealt, pw = pl.pallas_call(
        functools.partial(kernel, n, n_seq, cap),
        name="stem_and_deal",
        out_shape=(
            pltpu.VMEM((own, width + 128), BF16),
            pltpu.VMEM(patch_weight.shape, BF16),
        ),
        in_specs=[pl.BlockSpec(memory_space=pltpu.SMEM)] + [anywhere] * 9,
        out_specs=(vmem, pl.BlockSpec(memory_space=pltpu.VMEM)),
        scratch_shapes=[
            *(pltpu.VMEM(x.shape, x.dtype) for x in arrays),
            pltpu.VMEM((3, 8, 1024), BF16),
            pltpu.VMEM((3, 32, 128), BF16),
            pltpu.VMEM((3, 8, 128), BF16),
            pltpu.VMEM((n,) + keep_flags.shape, jnp.int32),
            pltpu.VMEM((3, 3, 80, 128), F32),
            pltpu.VMEM((128, 1152), F32),
            pltpu.VMEM((1280, 128), F32),
            pltpu.VMEM((M1, 384), BF16),
            pltpu.VMEM((384, 1280), BF16),
            pltpu.VMEM((10, M1, 128), F32),
            pltpu.VMEM((9, M2, 128), F32),
            pltpu.VMEM((2, 4, M3, 128), F32),
            pltpu.VMEM((2, n, cap, width), BF16),
            pltpu.VMEM((2, n, cap, width), BF16),
            dma((3,)), dma((3,)), dma((n,)), dma((n,)), dma((2, n)), dma((2, n)), dma((8,)), dma(()),
        ],
        compiler_params=pltpu.CompilerParams(
            collective_id=0, has_side_effects=True, vmem_limit_bytes=VMEM1
        ),
    )(
        owner_shift, *arrays, patch_weight,
    )
    placed = pl.pallas_call(
        project,
        name="project",
        out_shape=jax.ShapeDtypeStruct((own, embed), BF16),
        in_specs=[vmem] * 3,
        out_specs=vmem,
        compiler_params=pltpu.CompilerParams(vmem_limit_bytes=16 << 20),
    )(dealt, pw, patch_offset.reshape(-1, 128))
    return placed[None]


def solution(mesh):
    args = (P(None, "strip", "seq"), P("strip", "seq"), P("seq")) + (P(),) * 8
    return jax.shard_map(
        functools.partial(local, mesh.shape["strip"], mesh.shape["seq"]),
        mesh=mesh, in_specs=args, out_specs=P("seq", "strip", None), check_vma=False,
    )
```

time: 25.3 us -> 21.1 us (0.83)
  Pallas kernels: 22.9 us -> 20.2 us
  local copies, waits for them, and re-layouts: 1.62 us -> 0.01 us
    pallas_call x1, Pallas kernels: 22.9 us -> 18.9 us  [local(): pl.pallas_call(functools.partial(kernel, n, n_seq, cap), name='stem_and_d...]
    unnamed x1 -> x2, local copies, waits for them, and re-layouts: 1.62 us -> 0.01 us
    pallas_call x0 -> x1, Pallas kernels: none -> 1.34 us  [local(): pl.pallas_call(project, name='project', out_shape=jax.ShapeDtypeStruct((o...]
where the time goes in v1:
time: 21.1 us; the launch traced here: 20.9 us
  Pallas kernels  20.2 us (96%)
  between operations  0.68 us (3%)
    pallas_call x1, Pallas kernels, local(): pl.pallas_call(functools.partial(kernel, n, n_seq, cap), name='stem_and_d...  18.9 us
    pallas_call x1, Pallas kernels, local(): pl.pallas_call(project, name='project', out_shape=jax.ShapeDtypeStruct((o...  1.34 us

profile of v1, /device:TPU:0, one launch (start us, length us, event | category | flops | bytes accessed | tf_op | source)
XLA Modules:
  0.0 20.9 jit_solution(12803026590724480379)
XLA Ops:
  0.0 0.0 copy-start
  0.7 18.9 %stem_and_deal.1 = (bf16[64,1152]{1,0:T(8,128)(2,1)S(1)}, bf16[4,256,1536]{2,1,0:T(8,128)(2,1)S(1)}) custom-call(s32[1]{0:T(128)S(6)} %copy.12.shift_ref, bf16[3,32,1024]{2,1,0:T(8,128)(2,1)} %img_hbm.1, s32[2,64]{1,0:T(2,128)} %flag_hbm.1, bf16[9,3,64]{2,1,0:T(4,128)(2,1)} %bitcast.9, f32[1,64]{1,0:T(1,128)} %bitcast.11, bf16[9,64,128]{2,1,0:T(8,128)(2,1)} %bitcast.8, ...), custom_call_target="tpu_custom_call" | custom-call | tf_op jit(solution)/shard_map/stem_and_deal/pallas_call | solution.py:365
  19.6 0.0 copy-done
  19.6 1.3 %project.1 = bf16[64,1536]{1,0:T(8,128)(2,1)} custom-call(bf16[64,1152]{1,0:T(8,128)(2,1)S(1)} %get-tuple-element.7.dealt_ref, bf16[4,256,1536]{2,1,0:T(8,128)(2,1)S(1)} %get-tuple-element.8.pw_ref, f32[12,128]{1,0:T(8,128)S(1)} %bitcast.7), custom_call_target="tpu_custom_call" | custom-call | tf_op jit(solution)/shard_map/project/pallas_call | solution.py:398
Async XLA Ops:
  0.0 19.6 %copy-start = (f32[1536]{0:T(1024)S(1)}, f32[1536]{0:T(1024)}, u32[]{:S(2)}) copy-start(f32[1536]{0:T(1024)} %param.21) | copy-start | bytes 18436

commit v2 on v1

--- a/solution.py
+++ b/solution.py
@@ -130,19 +130,19 @@
         slab[40 * c + 8 : 40 * c + 40, 128:1152] = img_ref[c].astype(F32)
     slab_t[1152:1280, :] = jnp.zeros((128, 128), F32)
 
-    def fill_a1():
-        for t in range(9):
+    def fill_a1(tiles, rows):
+        for t in tiles:
             slab_t[128 * t : 128 * t + 128, :] = slab[:, 128 * t : 128 * t + 128].T
         for dx in range(3):
-            a1[:, 128 * dx : 128 * dx + 128] = slab_t[pl.ds(119 + dx, M1, stride=2), :].astype(BF16)
-
-    fill_a1()
+            a1[:rows, 128 * dx : 128 * dx + 128] = slab_t[pl.ds(119 + dx, rows, stride=2), :].astype(BF16)
+
+    fill_a1(range(9), M1)
     loads[2].wait()
     b1 = jnp.concatenate([b1_ref[...]] * 4, axis=1)
 
     def layer_one(t, rows):
         act = gelu(dot(a1[:rows], k1[:, 256 * t : 256 * t + 256]) + b1)
-        if t == 0 or rows < M1:
+        if t < 2 or rows < M1:
             sub1 = lax.broadcasted_iota(jnp.int32, (rows, 256), 0)
             ok = jnp.logical_or(inner_col, sub1 >= 4)
             if t == 0:
@@ -152,74 +152,80 @@
         s1[2 * t, :rows] = act[:, :128]
         s1[2 * t + 1, :rows] = act[:, 128:]
 
-    def layer_two(where, rows):
-        summed = None
-        for dx in range(3):
-            a = jnp.concatenate(
-                [
-                    jnp.concatenate(
-                        [s1[r + h, pl.ds(1 + dx, rows, stride=2), :] for r in where], axis=0
-                    ).astype(BF16)
-                    for h in range(2)
-                ],
-                axis=1,
-            )
-            w2 = jnp.concatenate(
-                [w2_ref[dx], w2_ref[3 + dx], w2_ref[6 + dx], jnp.zeros((64, 128), BF16)], axis=0
-            )
-            part = dot(a, w2)
-            summed = part if summed is None else summed + part
-        act = gelu(summed + b2_ref[...])
+    none = jnp.zeros((64, 128), BF16)
+
+    def tap2(dy, dx):
+        return none if dy is None else w2_ref[3 * dy + dx]
+
+    def layer_two(where, rows, pair):
+        tiles = (0, 1, 2) if pair else (0, 1)
+        order = [(h, dx) for dx in range(3) for h in (0, 1)] + [(2, dx) for dx in range(3) if pair]
+        a = jnp.concatenate(
+            [
+                jnp.concatenate(
+                    [s1[r + h, pl.ds(1 + dx, rows, stride=2), :] for r in where], axis=0
+                ).astype(BF16)
+                for h, dx in order
+            ],
+            axis=1,
+        )
+        first = {0: (0, 1), 1: (2, None), 2: (None, None)}
+        second = {0: (None, None), 1: (0, 1), 2: (2, None)}
+        w2 = []
+        for h, dx in order:
+            for part in range(2):
+                row = [tap2(first[h][part], dx)]
+                if pair:
+                    row.append(tap2(second[h][part], dx))
+                w2.append(jnp.concatenate(row, axis=1))
+        summed = dot(a, jnp.concatenate(w2, axis=0))
+        bias = jnp.concatenate([b2_ref[...]] * (2 if pair else 1), axis=1)
+        act = gelu(summed + bias)
         sub2 = lax.broadcasted_iota(jnp.int32, (rows, 128), 0)
         col_ok2 = jnp.logical_or(inner_col, sub2 >= 1)
         for k, r in enumerate(where):
-            one = act[rows * k : rows * k + rows]
-            if r < 2 or rows < M2:
-                ok = jnp.logical_and(col_ok2, inner_row) if r == 0 else col_ok2
-                one = jnp.where(ok, one, 0.0)
-            s2[r, :rows] = one
+            for more in range(2 if pair else 1):
+                one = act[rows * k : rows * k + rows, 128 * more : 128 * more + 128]
+                if r < 4 or rows < M2:
+                    ok = jnp.logical_and(col_ok2, inner_row) if r + more == 0 else col_ok2
+                    one = jnp.where(ok, one, 0.0)
+                s2[r + more, :rows] = one
 
     def layer_three(where, rows):
-        summed = None
-        for dy in range(3):
-            for dx in range(3):
-                a = jnp.concatenate(
+        taps = [(dy, dx) for dy in range(3) for dx in range(3)]
+        a = jnp.concatenate(
+            [
+                jnp.concatenate(
                     [s2[2 * r + dy, pl.ds(dx, rows, stride=2), :] for r in where], axis=0
                 ).astype(BF16)
-                part = dot_nt(a, w3_ref[3 * dy + dx])
-                summed = part if summed is None else summed + part
-        act = gelu(summed + b3_ref[...])
+                for dy, dx in taps
+            ],
+            axis=1,
+        )
+        w3 = jnp.concatenate([w3_ref[3 * dy + dx] for dy, dx in taps], axis=1)
+        act = gelu(dot_nt(a, w3) + b3_ref[...])
         for k, r in enumerate(where):
             s3[0, r, :rows] = act[rows * k : rows * k + rows, :128]
             s3[1, r, :rows] = act[rows * k : rows * k + rows, 128:]
 
-    for t in range(1, 5):
+    pl.when(late == 1)(enter)
+    for t in range(2, 5):
         layer_one(t, M1)
-    pl.when(late == 1)(enter)
     for load in loads[3:]:
         load.wait()
     pw_copy.start()
-    for r in range(4, 9):
-        layer_two([r], M2)
-    for r in (2, 3):
-        layer_three([r], M3)
+    layer_two([4], M2, True)
+    layer_two([6], M2, True)
+    layer_two([8], M2, False)
+    layer_three([2, 3], M3)
     pl.when(late == 0)(enter)
-    for r in (2, 3):
-        layer_two([r], M2)
-    layer_three([1], M3)
-
-    for buf, received, halo in zip((top, left, corner), receives, halos):
-        pl.when(received)(halo.wait_recv)
-
-        @pl.when(jnp.logical_not(received))
-        def _(buf=buf):
+
+    def receive(k, buf):
+        pl.when(receives[k])(halos[k].wait_recv)
+
+        @pl.when(jnp.logical_not(receives[k]))
+        def _():
             buf[...] = jnp.zeros_like(buf)
-
-    for c in range(3):
-        slab[40 * c : 40 * c + 8, 128:1152] = top[c].astype(F32)
-        slab[40 * c + 8 : 40 * c + 40, 0:128] = left[c].astype(F32)
-        slab[40 * c : 40 * c + 8, 0:128] = corner[c].astype(F32)
-    fill_a1()
 
     flags[me] = flag_ref[...]
     own = out_ref.shape[0]
@@ -272,9 +278,14 @@
         lax.fori_loop(1, n, send_rows, 0)
         got[pr, me] = sendbuf[pr, me]
 
-    for t in range(1, 5):
+    receive(1, left)
+    for c in range(3):
+        slab[40 * c + 8 : 40 * c + 40, 0:128] = left[c].astype(F32)
+    fill_a1(range(1), 16)
+    for t in range(2, 5):
         layer_one(t, 16)
-    layer_two(list(range(4, 9)), 8)
+    layer_two([4, 6], 8, True)
+    layer_two([8], 8, False)
     layer_three([2, 3], 8)
     near = lax.fori_loop(
         1 + late * me, me + 1 + late * (n - me - 1), near_flags, jnp.zeros(flag_ref.shape, jnp.int32)
@@ -284,12 +295,17 @@
     start = jnp.where(late == 1, n * own - near - mine[0] - mine[1], near + jnp.zeros((1, 1), F32))
     deal(1, (start + mine[0]).astype(jnp.int32))
 
-    layer_one(0, M1)
-    layer_two([0], M2)
-    layer_two([1], M2)
-    layer_two([2, 3], 8)
-    layer_three([0], M3)
-    layer_three([1], 8)
+    receive(0, top)
+    receive(2, corner)
+    for c in range(3):
+        slab[40 * c : 40 * c + 8, 128:1152] = top[c].astype(F32)
+        slab[40 * c : 40 * c + 8, 0:128] = corner[c].astype(F32)
+    fill_a1(range(9), M1)
+    for t in range(2):
+        layer_one(t, M1)
+    layer_two([0], M2, True)
+    layer_two([2], M2, True)
+    layer_three([0, 1], M3)
     deal(0, start.astype(jnp.int32))
 
     lax.fori_loop(me + 1 - late * me, n - late * (n - me - 1), far_flags, 0)

time: 21.1 us -> 19.3 us (0.915)
  Pallas kernels: 20.2 us -> 18.4 us
    pallas_call x1, Pallas kernels: 18.9 us -> 17.1 us  [local(): pl.pallas_call(functools.partial(kernel, n, n_seq, cap), name='stem_and_d...]
where the time goes in v2:
time: 19.3 us; the launch traced here: 19.1 us
  Pallas kernels  18.4 us (95%)
  between operations  0.68 us (4%)
    pallas_call x1, Pallas kernels, local(): pl.pallas_call(functools.partial(kernel, n, n_seq, cap), name='stem_and_d...  17.1 us
    pallas_call x1, Pallas kernels, local(): pl.pallas_call(project, name='project', out_shape=jax.ShapeDtypeStruct((o...  1.34 us

profile of v2, /device:TPU:0, one launch (start us, length us, event | category | flops | bytes accessed | tf_op | source)
XLA Modules:
  0.0 19.1 jit_solution(17574684575525571150)
XLA Ops:
  0.0 0.0 copy-start
  0.7 17.1 %stem_and_deal.1 = (bf16[64,1152]{1,0:T(8,128)(2,1)S(1)}, bf16[4,256,1536]{2,1,0:T(8,128)(2,1)S(1)}) custom-call(s32[1]{0:T(128)S(6)} %copy.12.shift_ref, bf16[3,32,1024]{2,1,0:T(8,128)(2,1)} %img_hbm.1, s32[2,64]{1,0:T(2,128)} %flag_hbm.1, bf16[9,3,64]{2,1,0:T(4,128)(2,1)} %bitcast.9, f32[1,64]{1,0:T(1,128)} %bitcast.11, bf16[9,64,128]{2,1,0:T(8,128)(2,1)} %bitcast.8, ...), custom_call_target="tpu_custom_call" | custom-call | tf_op jit(solution)/shard_map/stem_and_deal/pallas_call | solution.py:381
  17.7 0.0 copy-done
  17.7 1.3 %project.1 = bf16[64,1536]{1,0:T(8,128)(2,1)} custom-call(bf16[64,1152]{1,0:T(8,128)(2,1)S(1)} %get-tuple-element.7.dealt_ref, bf16[4,256,1536]{2,1,0:T(8,128)(2,1)S(1)} %get-tuple-element.8.pw_ref, f32[12,128]{1,0:T(8,128)S(1)} %bitcast.7), custom_call_target="tpu_custom_call" | custom-call | tf_op jit(solution)/shard_map/project/pallas_call | solution.py:414
Async XLA Ops:
  0.0 17.7 %copy-start = (f32[1536]{0:T(1024)S(1)}, f32[1536]{0:T(1024)}, u32[]{:S(2)}) copy-start(f32[1536]{0:T(1024)} %param.21) | copy-start | bytes 18436

commit v3 on v2

--- a/solution.py
+++ b/solution.py
@@ -11,7 +11,7 @@
 F32 = jnp.float32
 BF16 = jnp.bfloat16
 
-M1 = 560
+M1 = 528
 M2 = 272
 M3 = 128
 VMEM1 = 60000000
@@ -117,31 +117,39 @@
             for dy in range(3):
                 block = jnp.where(tap == dy, jnp.broadcast_to(tap_w[dy][c : c + 1], (8, 128)), block)
             band[dx, c, 40:48, :] = block
-        for q in range(10):
-            parts = [band[dx, c, 40 - 4 * q : 80 - 4 * q, :] for c in range(3)]
-            parts = jnp.concatenate(parts + [jnp.zeros((8, 128), F32)], axis=0)
-            k1[128 * dx : 128 * dx + 128, 128 * q : 128 * q + 128] = parts.astype(BF16)
-
-    slab[120:128, :] = jnp.zeros((8, 1152), F32)
-    slab[:120, 0:128] = jnp.zeros((120, 128), F32)
+    for q in range(6):
+        parts = [band[dx, c, 40 - 4 * q : 64 - 4 * q, :] for dx in range(3) for c in range(3)]
+        parts = jnp.concatenate(parts + [jnp.zeros((40, 128), F32)], axis=0)
+        k1[:, 128 * q : 128 * q + 128] = parts.astype(BF16)
+
+    slab[216:256, :] = jnp.zeros((40, 1280), F32)
+    slab[:72, 0:128] = jnp.zeros((72, 128), F32)
+    slab[:72, 1152:1280] = jnp.zeros((72, 128), F32)
+    slab_t[:, 1152:1280, :] = jnp.zeros((2, 128, 128), F32)
     loads[1].wait()
     for c in range(3):
-        slab[40 * c : 40 * c + 8, 128:1152] = jnp.zeros((8, 1024), F32)
-        slab[40 * c + 8 : 40 * c + 40, 128:1152] = img_ref[c].astype(F32)
-    slab_t[1152:1280, :] = jnp.zeros((128, 128), F32)
+        slab[24 * c : 24 * c + 24, 128:1152] = img_ref[c, 8:32].astype(F32)
 
     def fill_a1(tiles, rows):
-        for t in tiles:
-            slab_t[128 * t : 128 * t + 128, :] = slab[:, 128 * t : 128 * t + 128].T
-        for dx in range(3):
-            a1[:rows, 128 * dx : 128 * dx + 128] = slab_t[pl.ds(119 + dx, rows, stride=2), :].astype(BF16)
-
-    fill_a1(range(9), M1)
+        wide = min(1280, 128 * tiles + 128)
+        base = slab[:72, :wide]
+        for dx in range(1, 3):
+            moved = pltpu.roll(base, wide - dx, axis=1)
+            slab[72 * dx : 72 * dx + 72, : 128 * tiles] = moved[:, : 128 * tiles]
+        for t in range(tiles):
+            for k in range(2):
+                slab_t[k, 128 * t : 128 * t + 128, :] = slab[
+                    128 * k : 128 * k + 128, 128 * t : 128 * t + 128
+                ].T
+        for k in range(2):
+            a1[:rows, 128 * k : 128 * k + 128] = slab_t[k, pl.ds(119, rows, stride=2), :].astype(BF16)
+
+    fill_a1(9, M1)
     loads[2].wait()
     b1 = jnp.concatenate([b1_ref[...]] * 4, axis=1)
 
     def layer_one(t, rows):
-        act = gelu(dot(a1[:rows], k1[:, 256 * t : 256 * t + 256]) + b1)
+        act = gelu(dot(a1[:rows], k1[:, 256 * (t % 2 + t // 4 * 2) : 256 * (t % 2 + t // 4 * 2) + 256]) + b1)
         if t < 2 or rows < M1:
             sub1 = lax.broadcasted_iota(jnp.int32, (rows, 256), 0)
             ok = jnp.logical_or(inner_col, sub1 >= 4)
@@ -280,8 +288,8 @@
 
     receive(1, left)
     for c in range(3):
-        slab[40 * c + 8 : 40 * c + 40, 0:128] = left[c].astype(F32)
-    fill_a1(range(1), 16)
+        slab[24 * c : 24 * c + 24, 0:128] = left[c, 8:32].astype(F32)
+    fill_a1(1, 16)
     for t in range(2, 5):
         layer_one(t, 16)
     layer_two([4, 6], 8, True)
@@ -298,9 +306,11 @@
     receive(0, top)
     receive(2, corner)
     for c in range(3):
-        slab[40 * c : 40 * c + 8, 128:1152] = top[c].astype(F32)
-        slab[40 * c : 40 * c + 8, 0:128] = corner[c].astype(F32)
-    fill_a1(range(9), M1)
+        slab[24 * c : 24 * c + 8, 128:1152] = top[c].astype(F32)
+        slab[24 * c : 24 * c + 8, 0:128] = corner[c].astype(F32)
+        slab[24 * c + 8 : 24 * c + 24, 128:1152] = img_ref[c, 0:16].astype(F32)
+        slab[24 * c + 8 : 24 * c + 24, 0:128] = left[c, 0:16].astype(F32)
+    fill_a1(9, M1)
     for t in range(2):
         layer_one(t, M1)
     layer_two([0], M2, True)
@@ -394,11 +404,11 @@
             pltpu.VMEM((3, 8, 128), BF16),
             pltpu.VMEM((n,) + keep_flags.shape, jnp.int32),
             pltpu.VMEM((3, 3, 80, 128), F32),
-            pltpu.VMEM((128, 1152), F32),
-            pltpu.VMEM((1280, 128), F32),
-            pltpu.VMEM((M1, 384), BF16),
-            pltpu.VMEM((384, 1280), BF16),
-            pltpu.VMEM((10, M1, 128), F32),
+            pltpu.VMEM((256, 1280), F32),
+            pltpu.VMEM((2, 1280, 128), F32),
+            pltpu.VMEM((M1, 256), BF16),
+            pltpu.VMEM((256, 768), BF16),
+            pltpu.VMEM((10, 560, 128), F32),
             pltpu.VMEM((9, M2, 128), F32),
             pltpu.VMEM((2, 4, M3, 128), F32),
             pltpu.VMEM((2, n, cap, width), BF16),

time: 19.3 us -> 19.1 us (0.990)
  Pallas kernels: 18.4 us -> 18.1 us
    pallas_call x1, Pallas kernels: 17.1 us -> 16.8 us  [local(): pl.pallas_call(functools.partial(kernel, n, n_seq, cap), name='stem_and_d...]
where the time goes in v3:
time: 19.1 us; the launch traced here: 18.8 us
  Pallas kernels  18.1 us (95%)
  between operations  0.68 us (4%)
    pallas_call x1, Pallas kernels, local(): pl.pallas_call(functools.partial(kernel, n, n_seq, cap), name='stem_and_d...  16.8 us
    pallas_call x1, Pallas kernels, local(): pl.pallas_call(project, name='project', out_shape=jax.ShapeDtypeStruct((o...  1.34 us

profile of v3, /device:TPU:0, one launch (start us, length us, event | category | flops | bytes accessed | tf_op | source)
XLA Modules:
  0.0 18.8 jit_solution(1948995289690371596)
XLA Ops:
  0.0 0.0 copy-start
  0.7 16.8 %stem_and_deal.1 = (bf16[64,1152]{1,0:T(8,128)(2,1)S(1)}, bf16[4,256,1536]{2,1,0:T(8,128)(2,1)S(1)}) custom-call(s32[1]{0:T(128)S(6)} %copy.12.shift_ref, bf16[3,32,1024]{2,1,0:T(8,128)(2,1)} %img_hbm.1, s32[2,64]{1,0:T(2,128)} %flag_hbm.1, bf16[9,3,64]{2,1,0:T(4,128)(2,1)} %bitcast.9, f32[1,64]{1,0:T(1,128)} %bitcast.11, bf16[9,64,128]{2,1,0:T(8,128)(2,1)} %bitcast.8, ...), custom_call_target="tpu_custom_call" | custom-call | tf_op jit(solution)/shard_map/stem_and_deal/pallas_call | solution.py:391
  17.5 0.0 copy-done
  17.5 1.3 %project.1 = bf16[64,1536]{1,0:T(8,128)(2,1)} custom-call(bf16[64,1152]{1,0:T(8,128)(2,1)S(1)} %get-tuple-element.7.dealt_ref, bf16[4,256,1536]{2,1,0:T(8,128)(2,1)S(1)} %get-tuple-element.8.pw_ref, f32[12,128]{1,0:T(8,128)S(1)} %bitcast.7), custom_call_target="tpu_custom_call" | custom-call | tf_op jit(solution)/shard_map/project/pallas_call | solution.py:424
Async XLA Ops:
  0.0 17.5 %copy-start = (f32[1536]{0:T(1024)S(1)}, f32[1536]{0:T(1024)}, u32[]{:S(2)}) copy-start(f32[1536]{0:T(1024)} %param.21) | copy-start | bytes 18436

commit v4 on v3

--- a/solution.py
+++ b/solution.py
@@ -122,27 +122,21 @@
         parts = jnp.concatenate(parts + [jnp.zeros((40, 128), F32)], axis=0)
         k1[:, 128 * q : 128 * q + 128] = parts.astype(BF16)
 
-    slab[216:256, :] = jnp.zeros((40, 1280), F32)
-    slab[:72, 0:128] = jnp.zeros((72, 128), F32)
-    slab[:72, 1152:1280] = jnp.zeros((72, 128), F32)
-    slab_t[:, 1152:1280, :] = jnp.zeros((2, 128, 128), F32)
+    slab[:, 0:128] = jnp.zeros((72, 128), F32)
+    slab_t[...] = jnp.zeros_like(slab_t)
     loads[1].wait()
     for c in range(3):
         slab[24 * c : 24 * c + 24, 128:1152] = img_ref[c, 8:32].astype(F32)
 
     def fill_a1(tiles, rows):
-        wide = min(1280, 128 * tiles + 128)
-        base = slab[:72, :wide]
-        for dx in range(1, 3):
-            moved = pltpu.roll(base, wide - dx, axis=1)
-            slab[72 * dx : 72 * dx + 72, : 128 * tiles] = moved[:, : 128 * tiles]
         for t in range(tiles):
-            for k in range(2):
-                slab_t[k, 128 * t : 128 * t + 128, :] = slab[
-                    128 * k : 128 * k + 128, 128 * t : 128 * t + 128
-                ].T
-        for k in range(2):
-            a1[:rows, 128 * k : 128 * k + 128] = slab_t[k, pl.ds(119, rows, stride=2), :].astype(BF16)
+            slab_t[128 * t : 128 * t + 128, 0:72] = slab[:, 128 * t : 128 * t + 128].T
+        one, two, three = [slab_t[pl.ds(119 + dx, rows, stride=2), :] for dx in range(3)]
+        two = pltpu.roll(two, 72, axis=1)
+        three = pltpu.roll(three, 16, axis=1)
+        lane = lax.broadcasted_iota(jnp.int32, (rows, 128), 1)
+        a1[:rows, 0:128] = jnp.where(lane < 72, one, two).astype(BF16)
+        a1[:rows, 128:256] = jnp.where(lane < 16, two, three).astype(BF16)
 
     fill_a1(9, M1)
     loads[2].wait()
@@ -225,7 +219,6 @@
     layer_two([4], M2, True)
     layer_two([6], M2, True)
     layer_two([8], M2, False)
-    layer_three([2, 3], M3)
     pl.when(late == 0)(enter)
 
     def receive(k, buf):
@@ -294,7 +287,7 @@
         layer_one(t, 16)
     layer_two([4, 6], 8, True)
     layer_two([8], 8, False)
-    layer_three([2, 3], 8)
+    layer_three([2, 3], M3)
     near = lax.fori_loop(
         1 + late * me, me + 1 + late * (n - me - 1), near_flags, jnp.zeros(flag_ref.shape, jnp.int32)
     )
@@ -404,8 +397,8 @@
             pltpu.VMEM((3, 8, 128), BF16),
             pltpu.VMEM((n,) + keep_flags.shape, jnp.int32),
             pltpu.VMEM((3, 3, 80, 128), F32),
-            pltpu.VMEM((256, 1280), F32),
-            pltpu.VMEM((2, 1280, 128), F32),
+            pltpu.VMEM((72, 1152), F32),
+            pltpu.VMEM((1280, 128), F32),
             pltpu.VMEM((M1, 256), BF16),
             pltpu.VMEM((256, 768), BF16),
             pltpu.VMEM((10, 560, 128), F32),

time: 19.1 us -> 19 us (level)
  no operation moved by 1% of the time
where the time goes in v4:
time: 19 us; the launch traced here: 18.8 us
  Pallas kernels  18.1 us (95%)
  between operations  0.68 us (4%)
    pallas_call x1, Pallas kernels, local(): pl.pallas_call(functools.partial(kernel, n, n_seq, cap), name='stem_and_d...  16.7 us
    pallas_call x1, Pallas kernels, local(): pl.pallas_call(project, name='project', out_shape=jax.ShapeDtypeStruct((o...  1.34 us

profile of v4, /device:TPU:0, one launch (start us, length us, event | category | flops | bytes accessed | tf_op | source)
XLA Modules:
  0.0 18.8 jit_solution(8463244145825417772)
XLA Ops:
  0.0 0.0 copy-start
  0.7 16.7 %stem_and_deal.1 = (bf16[64,1152]{1,0:T(8,128)(2,1)S(1)}, bf16[4,256,1536]{2,1,0:T(8,128)(2,1)S(1)}) custom-call(s32[1]{0:T(128)S(6)} %copy.12.shift_ref, bf16[3,32,1024]{2,1,0:T(8,128)(2,1)} %img_hbm.1, s32[2,64]{1,0:T(2,128)} %flag_hbm.1, bf16[9,3,64]{2,1,0:T(4,128)(2,1)} %bitcast.9, f32[1,64]{1,0:T(1,128)} %bitcast.11, bf16[9,64,128]{2,1,0:T(8,128)(2,1)} %bitcast.8, ...), custom_call_target="tpu_custom_call" | custom-call | tf_op jit(solution)/shard_map/stem_and_deal/pallas_call | solution.py:384
  17.4 0.0 copy-done
  17.4 1.3 %project.1 = bf16[64,1536]{1,0:T(8,128)(2,1)} custom-call(bf16[64,1152]{1,0:T(8,128)(2,1)S(1)} %get-tuple-element.7.dealt_ref, bf16[4,256,1536]{2,1,0:T(8,128)(2,1)S(1)} %get-tuple-element.8.pw_ref, f32[12,128]{1,0:T(8,128)S(1)} %bitcast.7), custom_call_target="tpu_custom_call" | custom-call | tf_op jit(solution)/shard_map/project/pallas_call | solution.py:417
Async XLA Ops:
  0.0 17.4 %copy-start = (f32[1536]{0:T(1024)S(1)}, f32[1536]{0:T(1024)}, u32[]{:S(2)}) copy-start(f32[1536]{0:T(1024)} %param.21) | copy-start | bytes 18436

commit v5 on v4

--- a/solution.py
+++ b/solution.py
@@ -359,10 +359,8 @@
     filled = jnp.concatenate([filled, filled], axis=1)
     for t in range(6):
         cut = slice(256 * t, 256 * t + 256)
-        summed = None
-        for k in range(4):
-            part = dot(dealt_ref[:, 256 * k : 256 * k + 256], pw_ref[k, :, cut])
-            summed = part if summed is None else summed + part
+        weight = jnp.concatenate([pw_ref[k, :, cut] for k in range(4)], axis=0)
+        summed = dot(dealt_ref[:, :width], weight)
         bias = jnp.concatenate([pb_ref[2 * t : 2 * t + 1], pb_ref[2 * t + 1 : 2 * t + 2]], axis=1)
         out_ref[:, cut] = jnp.where(filled > 0.5, summed + bias, 0.0).astype(BF16)
 

time: 19 us -> 19 us (level)
  no operation moved by 1% of the time
where the time goes in v5:
time: 19 us; the launch traced here: 18.8 us
  Pallas kernels  18.1 us (95%)
  between operations  0.68 us (4%)
    pallas_call x1, Pallas kernels, local(): pl.pallas_call(functools.partial(kernel, n, n_seq, cap), name='stem_and_d...  16.7 us
    pallas_call x1, Pallas kernels, local(): pl.pallas_call(project, name='project', out_shape=jax.ShapeDtypeStruct((o...  1.34 us

profile of v5, /device:TPU:0, one launch (start us, length us, event | category | flops | bytes accessed | tf_op | source)
XLA Modules:
  0.0 18.8 jit_solution(100700146342596222)
XLA Ops:
  0.0 0.0 copy-start
  0.7 16.7 %stem_and_deal.1 = (bf16[64,1152]{1,0:T(8,128)(2,1)S(1)}, bf16[4,256,1536]{2,1,0:T(8,128)(2,1)S(1)}) custom-call(s32[1]{0:T(128)S(6)} %copy.12.shift_ref, bf16[3,32,1024]{2,1,0:T(8,128)(2,1)} %img_hbm.1, s32[2,64]{1,0:T(2,128)} %flag_hbm.1, bf16[9,3,64]{2,1,0:T(4,128)(2,1)} %bitcast.9, f32[1,64]{1,0:T(1,128)} %bitcast.11, bf16[9,64,128]{2,1,0:T(8,128)(2,1)} %bitcast.8, ...), custom_call_target="tpu_custom_call" | custom-call | tf_op jit(solution)/shard_map/stem_and_deal/pallas_call | solution.py:382
  17.4 0.0 copy-done
  17.4 1.3 %project.1 = bf16[64,1536]{1,0:T(8,128)(2,1)} custom-call(bf16[64,1152]{1,0:T(8,128)(2,1)S(1)} %get-tuple-element.7.dealt_ref, bf16[4,256,1536]{2,1,0:T(8,128)(2,1)S(1)} %get-tuple-element.8.pw_ref, f32[12,128]{1,0:T(8,128)S(1)} %bitcast.7), custom_call_target="tpu_custom_call" | custom-call | tf_op jit(solution)/shard_map/project/pallas_call | solution.py:415
Async XLA Ops:
  0.0 17.4 %copy-start = (f32[1536]{0:T(1024)S(1)}, f32[1536]{0:T(1024)}, u32[]{:S(2)}) copy-start(f32[1536]{0:T(1024)} %param.21) | copy-start | bytes 18436

commit v6 on v5

--- a/solution.py
+++ b/solution.py
@@ -273,7 +273,7 @@
         sendbuf[pr] = rows.reshape(n, cap, rows.shape[1]).astype(BF16)
 
         def send_rows(i, c):
-            row_copy(pr, i, me).start()
+            row_copy(pr, late * i + (1 - late) * (n - i), me).start()
             return c
 
         lax.fori_loop(1, n, send_rows, 0)

time: 19 us -> 19.1 us (level)
  no operation moved by 1% of the time
where the time goes in v6:
time: 19.1 us; the launch traced here: 18.9 us
  Pallas kernels  18.2 us (95%)
  between operations  0.68 us (4%)
    pallas_call x1, Pallas kernels, local(): pl.pallas_call(functools.partial(kernel, n, n_seq, cap), name='stem_and_d...  16.8 us
    pallas_call x1, Pallas kernels, local(): pl.pallas_call(project, name='project', out_shape=jax.ShapeDtypeStruct((o...  1.34 us

profile of v6, /device:TPU:0, one launch (start us, length us, event | category | flops | bytes accessed | tf_op | source)
XLA Modules:
  0.0 18.9 jit_solution(17958072277515522369)
XLA Ops:
  0.0 0.0 copy-start
  0.7 16.8 %stem_and_deal.1 = (bf16[64,1152]{1,0:T(8,128)(2,1)S(1)}, bf16[4,256,1536]{2,1,0:T(8,128)(2,1)S(1)}) custom-call(s32[1]{0:T(128)S(6)} %copy.12.shift_ref, bf16[3,32,1024]{2,1,0:T(8,128)(2,1)} %img_hbm.1, s32[2,64]{1,0:T(2,128)} %flag_hbm.1, bf16[9,3,64]{2,1,0:T(4,128)(2,1)} %bitcast.9, f32[1,64]{1,0:T(1,128)} %bitcast.11, bf16[9,64,128]{2,1,0:T(8,128)(2,1)} %bitcast.8, ...), custom_call_target="tpu_custom_call" | custom-call | tf_op jit(solution)/shard_map/stem_and_deal/pallas_call | solution.py:382
  17.5 0.0 copy-done
  17.5 1.3 %project.1 = bf16[64,1536]{1,0:T(8,128)(2,1)} custom-call(bf16[64,1152]{1,0:T(8,128)(2,1)S(1)} %get-tuple-element.7.dealt_ref, bf16[4,256,1536]{2,1,0:T(8,128)(2,1)S(1)} %get-tuple-element.8.pw_ref, f32[12,128]{1,0:T(8,128)S(1)} %bitcast.7), custom_call_target="tpu_custom_call" | custom-call | tf_op jit(solution)/shard_map/project/pallas_call | solution.py:415
Async XLA Ops:
  0.0 17.5 %copy-start = (f32[1536]{0:T(1024)S(1)}, f32[1536]{0:T(1024)}, u32[]{:S(2)}) copy-start(f32[1536]{0:T(1024)} %param.21) | copy-start | bytes 18436
